TPU v7x, 32 devices: a whole 2x2x4 slice. The times are simulated.
32 devices in a mesh: expert: 8 (over z, y), hidden: 4 (over x, core).
Axes of the slice: x: 2, y: 2, z: 4, core: 2. Of those that a mesh axis runs over, the one named last changes fastest.
Arguments:
- tokens: bfloat16 [2, 6144, 768], P(None, 'expert'), may hold values from -6 to 6
- doc_ids: int32 [2, 8, 768], P(None, 'expert'), may hold values from 0 to 3, never falling along the last dimension, each value on 1 to 384 neighbouring positions
- pad_mask: int32 [2, 6144], P(None, 'expert'), may hold values 0 or 1
- norm1_gain: float32 [768], replicated, may hold values from 0.5 to 1.5
- norm1_bias: float32 [768], replicated, may hold values from -1 to 1
- qkv_weight: bfloat16 [3, 768, 768], P(None, None, 'hidden'), may hold values from -0.3125 to 0.3125
- out_weight: bfloat16 [768, 768], P('hidden'), may hold values from -0.875 to 0.875
- norm2_gain: float32 [768], replicated, may hold values from 0.5 to 1.5
- norm2_bias: float32 [768], replicated, may hold values from -1 to 1
- router: bfloat16 [768, 8], replicated, may hold values from -0.15625 to 0.15625
- routes: int32 [2, 6144, 2], P(None, 'expert'), may hold values from 0 to 7, all different within a row; in each aligned block of 768 rows (0 to 767, 768 to 1535, ..., all dimensions but the last counted through in order) at most 384 rows name the same one
- up_weight: bfloat16 [8, 768, 3072], P('expert', None, 'hidden'), may hold values from -0.21875 to 0.21875
- down_weight: bfloat16 [8, 768, 3072], P('expert', None, 'hidden'), may hold values from -0.15625 to 0.15625
- cotangent: bfloat16 [2, 6144, 768], P(None, 'expert'), may hold values from -6 to 6
Outputs:
- block_out: float32 [2, 6144, 768], P(None, 'expert')
- grad_tokens: float32 [2, 6144, 768], P(None, 'expert')
- grad_norm1_gain: float32 [768], replicated
- grad_norm1_bias: float32 [768], replicated
- grad_qkv: float32 [3, 768, 768], P(None, None, 'hidden')
- grad_out: float32 [768, 768], P('hidden')
- grad_norm2_gain: float32 [768], replicated
- grad_norm2_bias: float32 [768], replicated
- grad_router: float32 [768, 8], replicated
- grad_up: float32 [4, 768, 3072], P(None, 'expert', 'hidden')
- grad_down: float32 [4, 768, 3072], P(None, 'expert', 'hidden')
Inputs may be any that keep to these rules, and one draw needn't show every extreme that they name: `routes`: each token names 2 different experts. In each micro-batch the tokens of one pack name any one expert at most 384 times, a bound that some block reaches. `doc_ids`: within a pack document numbers never fall; each document covers 1 to 384 consecutive tokens, and some covers exactly 384. `pad_mask`: 1 marks a real token, 0 a padding token.
All inputs are finite; a program needn't handle non-finite values. No bound on the sum of `pad_mask` on one device may be relied on, other than what follows from the above.
Results may differ from a plain program's by a relative error of at most 0.028.
Values may be sent and summed in bfloat16 or wider, within the bound.
No kernel may reach another device: no remote copies, remote signals or barrier semaphores. Data moves between devices by JAX's collectives and lax.ppermute only.
A program may use at most 256 MiB of HBM per device.

v0:
```python
import jax
import jax.numpy as jnp
from jax import lax
from jax.sharding import PartitionSpec as P

HEAD_DIM = 64
EPSILON = 1e-05
PRECISE = lax.Precision.HIGHEST
MASKED = -1e30


def layer_norm(values, norm_gain, norm_bias):
    centre = values - jnp.mean(values, -1, keepdims=True)
    spread = jnp.mean(centre * centre, -1, keepdims=True)
    return centre * lax.rsqrt(spread + EPSILON) * norm_gain + norm_bias


def gelu_tanh(values):
    return jax.nn.gelu(values, approximate=True)


def visible(doc_row, pad_row):
    total_rows = doc_row.shape[0]
    query_pos = jnp.arange(total_rows)[:, None]
    key_pos = jnp.arange(total_rows)[None, :]
    same_doc = doc_row[:, None] == doc_row[None, :]
    is_real = (pad_row[None, :] == 1) | (query_pos == key_pos)
    return (key_pos <= query_pos) & same_doc & is_real


def slot_tables(route_rows, experts, capacity):
    flat_routes = route_rows.reshape(-1)
    onehot = (flat_routes[:, None] == jnp.arange(experts, dtype=jnp.int32)[None, :]).astype(
        jnp.int32
    )
    before = jnp.cumsum(onehot, 0) - onehot
    placed = jnp.sum(before * onehot, 1)
    slot_index = flat_routes * capacity + placed
    total_rows = flat_routes.shape[0]
    source = (
        jnp.full((experts * capacity,), total_rows, jnp.int32)
        .at[slot_index]
        .set(jnp.arange(total_rows, dtype=jnp.int32))
    )
    return (slot_index, source)


def masked_scores(queries, key_rows, allowed, score_scale):
    scores = (
        jnp.einsum("qhd,khd->hqk", queries, key_rows, preferred_element_type=jnp.float32)
        * score_scale
    )
    return jnp.where(allowed[None], scores, MASKED)


def attend_forward(queries, key_rows, value_rows, allowed, score_scale):
    scores = masked_scores(queries, key_rows, allowed, score_scale)
    row_peak = jnp.max(scores, -1, keepdims=True)
    exponent = jnp.exp(scores - row_peak)
    row_total = jnp.sum(exponent, -1, keepdims=True)
    attn_weights = (exponent / row_total).astype(jnp.bfloat16)
    output = jnp.einsum(
        "hqk,khd->qhd", attn_weights, value_rows, preferred_element_type=jnp.float32
    )
    return (output, row_peak + jnp.log(row_total))


def attend_backward(queries, key_rows, value_rows, allowed, score_scale, log_total, heads_grad):
    scores = masked_scores(queries, key_rows, allowed, score_scale)
    attn_weights = jnp.exp(scores - log_total)
    weight_grad = jnp.einsum(
        "qhd,khd->hqk", heads_grad, value_rows, preferred_element_type=jnp.float32
    )
    row_delta = jnp.sum(attn_weights * weight_grad, -1, keepdims=True)
    score_grad = (attn_weights * (weight_grad - row_delta)).astype(jnp.bfloat16)
    query_grad = (
        jnp.einsum("hqk,khd->qhd", score_grad, key_rows, preferred_element_type=jnp.float32)
        * score_scale
    )
    key_grad = (
        jnp.einsum("hqk,qhd->khd", score_grad, queries, preferred_element_type=jnp.float32)
        * score_scale
    )
    value_grad = jnp.einsum(
        "hqk,qhd->khd",
        attn_weights.astype(jnp.bfloat16),
        heads_grad,
        preferred_element_type=jnp.float32,
    )
    return (query_grad, key_grad, value_grad)


def shards(
    tokens,
    doc_ids,
    pad_mask,
    norm1_gain,
    norm1_bias,
    qkv_weight,
    out_weight,
    norm2_gain,
    norm2_bias,
    router,
    routes,
    up_weight,
    down_weight,
    cotangent,
):
    micro_count, row_count, feat_width = tokens.shape
    expert_count = router.shape[1]
    top_count = routes.shape[2]
    capacity = 2 * row_count * top_count // expert_count
    local_heads = qkv_weight.shape[2] // HEAD_DIM
    score_scale = HEAD_DIM ** (-0.5)
    trainable = lax.axis_index("expert") >= lax.axis_size("expert") // 2
    up_local = up_weight[0]
    down_local = down_weight[0]
    router_wide = router.astype(jnp.float32)
    zero_row = jnp.zeros((1, feat_width), jnp.bfloat16)
    grad_qkv = jnp.zeros(qkv_weight.shape, jnp.float32)
    grad_proj = jnp.zeros(out_weight.shape, jnp.float32)
    grad_router = jnp.zeros(router.shape, jnp.float32)
    gain1_total = jnp.zeros((feat_width,), jnp.float32)
    bias1_total = jnp.zeros((feat_width,), jnp.float32)
    gain2_total = jnp.zeros((feat_width,), jnp.float32)
    bias2_total = jnp.zeros((feat_width,), jnp.float32)
    expert_acc = (jnp.zeros(up_local.shape, jnp.float32), jnp.zeros(down_local.shape, jnp.float32))
    outputs = []
    input_grads = []
    for micro_idx in range(micro_count):
        inputs = tokens[micro_idx].astype(jnp.float32)
        allowed = visible(doc_ids[micro_idx, 0], pad_mask[micro_idx])
        normed1, norm1_pull = jax.vjp(layer_norm, inputs, norm1_gain, norm1_bias)
        attn_in = normed1.astype(jnp.bfloat16)
        projected = jnp.einsum(
            "rd,cdf->crf", attn_in, qkv_weight, preferred_element_type=jnp.float32
        ).astype(jnp.bfloat16)
        head_view = projected.reshape(3, row_count, local_heads, HEAD_DIM)
        queries, key_rows, value_rows = (head_view[0], head_view[1], head_view[2])
        heads_out, log_total = attend_forward(queries, key_rows, value_rows, allowed, score_scale)
        heads_low = heads_out.reshape(row_count, -1).astype(jnp.bfloat16)
        attn_term = jnp.dot(heads_low, out_weight, preferred_element_type=jnp.float32)
        attention = lax.psum(attn_term.astype(jnp.bfloat16), "hidden").astype(jnp.float32)
        residual = inputs + attention
        normed2, norm2_pull = jax.vjp(layer_norm, residual, norm2_gain, norm2_bias)
        moe_in = normed2.astype(jnp.bfloat16)
        logits = jnp.dot(moe_in, router, preferred_element_type=jnp.float32)
        route_rows = routes[micro_idx]
        picker = (
            route_rows[:, :, None] == jnp.arange(expert_count, dtype=jnp.int32)[None, None, :]
        ).astype(jnp.float32)
        chosen = jnp.sum(picker * logits[:, None, :], -1)
        gate_vals = jax.nn.softmax(chosen, -1)
        slot_index, source = slot_tables(route_rows, expert_count, capacity)
        padded_in = jnp.concatenate([moe_in, zero_row], 0)
        send_rows = padded_in[source // top_count].reshape(expert_count, capacity, feat_width)
        received = lax.all_to_all(
            send_rows, "expert", split_axis=0, concat_axis=0, tiled=True
        ).reshape(-1, feat_width)
        hidden_pre = jnp.dot(received, up_local, preferred_element_type=jnp.float32)
        hidden_act = gelu_tanh(hidden_pre).astype(jnp.bfloat16)
        slice_out = jnp.einsum(
            "rf,df->rd", hidden_act, down_local, preferred_element_type=jnp.float32
        )
        summed = lax.psum(slice_out.astype(jnp.bfloat16), "hidden")
        returned = lax.all_to_all(
            summed.reshape(expert_count, capacity, feat_width),
            "expert",
            split_axis=0,
            concat_axis=0,
            tiled=True,
        )
        flat_back = jnp.concatenate([returned.reshape(-1, feat_width), zero_row], 0)
        expert_rows = flat_back[slot_index].reshape(row_count, top_count, feat_width)
        expert_wide = expert_rows.astype(jnp.float32)
        mixture = jnp.sum(gate_vals[:, :, None] * expert_wide, 1)
        outputs.append(residual + mixture)
        upstream = cotangent[micro_idx].astype(jnp.float32)
        expert_grad = (gate_vals[:, :, None] * upstream[:, None, :]).astype(jnp.bfloat16)
        gate_grad = jnp.sum(upstream[:, None, :] * expert_wide, -1)
        chosen_grad = gate_vals * (gate_grad - jnp.sum(gate_vals * gate_grad, -1, keepdims=True))
        logit_grad = jnp.sum(picker * chosen_grad[:, :, None], 1)
        padded_grad = jnp.concatenate([expert_grad.reshape(-1, feat_width), zero_row], 0)
        send_grad = padded_grad[source].reshape(expert_count, capacity, feat_width)
        grad_rows = lax.all_to_all(
            send_grad, "expert", split_axis=0, concat_axis=0, tiled=True
        ).reshape(-1, feat_width)
        act_grad = jnp.dot(grad_rows, down_local, preferred_element_type=jnp.float32)
        gelu_grad = jax.vjp(gelu_tanh, hidden_pre)[1](act_grad)[0]
        pre_grad = gelu_grad.astype(jnp.bfloat16)
        in_term = jnp.einsum("rf,df->rd", pre_grad, up_local, preferred_element_type=jnp.float32)
        in_summed = lax.psum(in_term.astype(jnp.bfloat16), "hidden")
        in_back = lax.all_to_all(
            in_summed.reshape(expert_count, capacity, feat_width),
            "expert",
            split_axis=0,
            concat_axis=0,
            tiled=True,
        )
        flat_in = jnp.concatenate([in_back.reshape(-1, feat_width), zero_row], 0)
        copies_low = flat_in[slot_index].reshape(row_count, top_count, feat_width)
        copies_grad = copies_low.astype(jnp.float32)
        normed2_grad = jnp.sum(copies_grad, 1) + jnp.dot(
            logit_grad, router_wide.T, precision=PRECISE
        )

        def expert_update(acc_pair):
            return (
                acc_pair[0]
                + jnp.einsum("rd,rf->df", received, pre_grad, preferred_element_type=jnp.float32),
                acc_pair[1]
                + jnp.einsum(
                    "rd,rf->df", grad_rows, hidden_act, preferred_element_type=jnp.float32
                ),
            )

        def expert_keep(acc_pair):
            return acc_pair

        expert_acc = lax.cond(trainable, expert_update, expert_keep, expert_acc)
        grad_router = grad_router + jnp.dot(
            moe_in.astype(jnp.float32).T, logit_grad, precision=PRECISE
        )
        resid_grad, gain2_grad, bias2_grad = norm2_pull(normed2_grad)
        gain2_total = gain2_total + gain2_grad
        bias2_total = bias2_total + bias2_grad
        resid_grad = upstream + resid_grad
        attn_grad = resid_grad.astype(jnp.bfloat16)
        grad_proj = grad_proj + jnp.einsum(
            "rf,rd->fd", heads_low, attn_grad, preferred_element_type=jnp.float32
        )
        heads_grad = jnp.einsum(
            "rd,fd->rf", attn_grad, out_weight, preferred_element_type=jnp.float32
        ).astype(jnp.bfloat16)
        query_grad, key_grad, value_grad = attend_backward(
            queries,
            key_rows,
            value_rows,
            allowed,
            score_scale,
            log_total,
            heads_grad.reshape(row_count, local_heads, HEAD_DIM),
        )
        qkv_grad = (
            jnp.stack([query_grad, key_grad, value_grad])
            .reshape(3, row_count, -1)
            .astype(jnp.bfloat16)
        )
        grad_qkv = grad_qkv + jnp.einsum(
            "rd,crf->cdf", attn_in, qkv_grad, preferred_element_type=jnp.float32
        )
        normed1_term = jnp.einsum(
            "crf,cdf->rd", qkv_grad, qkv_weight, preferred_element_type=jnp.float32
        )
        normed1_grad = lax.psum(normed1_term.astype(jnp.bfloat16), "hidden").astype(jnp.float32)
        input_grad, gain1_grad, bias1_grad = norm1_pull(normed1_grad)
        gain1_total = gain1_total + gain1_grad
        bias1_total = bias1_total + bias1_grad
        input_grads.append(resid_grad + input_grad)
    reduced = (
        lax.psum(gain1_total.astype(jnp.bfloat16), "expert").astype(jnp.float32),
        lax.psum(bias1_total.astype(jnp.bfloat16), "expert").astype(jnp.float32),
        lax.psum(grad_qkv.astype(jnp.bfloat16), "expert").astype(jnp.float32),
        lax.psum(grad_proj.astype(jnp.bfloat16), "expert").astype(jnp.float32),
        lax.psum(gain2_total.astype(jnp.bfloat16), "expert").astype(jnp.float32),
        lax.psum(bias2_total.astype(jnp.bfloat16), "expert").astype(jnp.float32),
        lax.psum(grad_router.astype(jnp.bfloat16), "expert").astype(jnp.float32),
    )
    expert_parts = (
        lax.all_to_all(
            expert_acc[0][None].astype(jnp.bfloat16),
            "expert",
            split_axis=1,
            concat_axis=0,
            tiled=True,
        ).astype(jnp.float32),
        lax.all_to_all(
            expert_acc[1][None].astype(jnp.bfloat16),
            "expert",
            split_axis=1,
            concat_axis=0,
            tiled=True,
        ).astype(jnp.float32),
    )
    half_count = expert_count // 2
    return (
        jnp.stack(outputs),
        jnp.stack(input_grads),
        reduced[0],
        reduced[1],
        reduced[2],
        reduced[3],
        reduced[4],
        reduced[5],
        reduced[6],
        expert_parts[0][half_count:],
        expert_parts[1][half_count:],
    )


def solution(mesh):
    placed = (
        P(None, "expert", None),
        P(None, "expert", None),
        P(None, "expert"),
        P(),
        P(),
        P(None, None, "hidden"),
        P("hidden", None),
        P(),
        P(),
        P(),
        P(None, "expert", None),
        P("expert", None, "hidden"),
        P("expert", None, "hidden"),
        P(None, "expert", None),
    )
    return jax.shard_map(
        shards,
        mesh=mesh,
        in_specs=placed,
        out_specs=(
            P(None, "expert", None),
            P(None, "expert", None),
            P(),
            P(),
            P(None, None, "hidden"),
            P("hidden", None),
            P(),
            P(),
            P(),
            P(None, "expert", "hidden"),
            P(None, "expert", "hidden"),
        ),
        check_vma=False,
    )
```

profile of v0, /device:TPU:0, one launch (start us, length us, event | category | flops | bytes accessed | tf_op | source)
XLA Modules:
  0.0 1665.4 jit_solution(2692091185587568231)
XLA Ops:
  46.8 17.9 %all-reduce.18.cloned.1.call-done = bf16[768,768]{1,0:T(8,128)(2,1)} async-done(((bf16[768,768]{1,0:T(8,128)(2,1)}), bf16[768,768]{1,0:T(8,128)(2,1)}) %all-reduce.18.cloned.1.call-update) | async-done | bytes 1179664 | tf_op jit(solution)/shard_map/psum | solution.py:143
  82.5 5.6 mul.541
  88.1 6.9 mul.542
  96.9 7.0 scatter_custom_fusion
  105.3 10.1 all-reduce.20.cloned.1.call-done
  128.2 14.5 gather_fusion.4
  142.7 5.6 all-to-all-start.4
  153.0 6.2 scatter_custom_fusion.1
  159.9 14.5 gather_fusion.2
  174.4 78.2 %all-to-all-done.4 = bf16[8,384,768]{2,1,0:T(8,128)(2,1)} async-done(((bf16[8,384,768]{2,1,0:T(8,128)(2,1)}), bf16[8,384,768]{2,1,0:T(8,128)(2,1)}, u32[]{:S(2)}, u32[]{:S(2)}) %all-to-all-start.4) | async-done | bytes 4718624 | tf_op jit(solution)/shard_map/all_to_all | solution.py:185
  257.5 14.5 gather_fusion
  272.1 89.1 %all-to-all-done.2 = bf16[8,384,768]{2,1,0:T(8,128)(2,1)} async-done(((bf16[8,384,768]{2,1,0:T(8,128)(2,1)}), bf16[8,384,768]{2,1,0:T(8,128)(2,1)}, u32[]{:S(2)}, u32[]{:S(2)}) %all-to-all-start.2) | async-done | bytes 4718624 | tf_op jit(solution)/shard_map/all_to_all | solution.py:157
  369.7 7.0 mul.579
  382.2 14.6 gather_fusion.6
  396.8 72.8 %all-to-all-done = bf16[8,384,768]{2,1,0:T(8,128)(2,1)} async-done(((bf16[8,384,768]{2,1,0:T(8,128)(2,1)}), bf16[8,384,768]{2,1,0:T(8,128)(2,1)}, u32[]{:S(2)}, u32[]{:S(2)}) %all-to-all-start) | async-done | bytes 4718624 | tf_op jit(solution)/shard_map/all_to_all | solution.py:157
  474.4 7.7 multiply_convert_fusion.1
  482.1 12.1 fusion.6
  494.1 5.6 convolution_convert_fusion.1
  505.3 10.1 multiply_convert_fusion
  515.4 62.6 %all-to-all-done.6 = bf16[8,384,768]{2,1,0:T(8,128)(2,1)} async-done(((bf16[8,384,768]{2,1,0:T(8,128)(2,1)}), bf16[8,384,768]{2,1,0:T(8,128)(2,1)}, u32[]{:S(2)}, u32[]{:S(2)}) %all-to-all-start.6) | async-done | bytes 4718624 | tf_op jit(solution)/shard_map/all_to_all | solution.py:185
  578.0 11.9 fusion.13
  589.9 5.6 convolution_convert_fusion
  595.5 5.6 convolution_convert_fusion.2
  609.3 7.8 reduce.30
  618.3 32.7 %all-to-all-start.8 = ((bf16[8,2,36864]{2,1,0:T(2,128)(2,1)}), bf16[8,2,36864]{2,1,0:T(2,128)(2,1)}, u32[]{:S(2)}, u32[]{:S(2)}) async-start(bf16[8,2,36864]{2,1,0:T(2,128)(2,1)} %reshape.916), calls=%async_computation.8 | async-start | bytes 2359296 | tf_op jit(solution)/shard_map/all_to_all | solution.py:270
  652.9 7.8 reduce.31
  661.1 18.7 %all-to-all-done.8 = bf16[8,2,36864]{2,1,0:T(2,128)(2,1)} async-done(((bf16[8,2,36864]{2,1,0:T(2,128)(2,1)}), bf16[8,2,36864]{2,1,0:T(2,128)(2,1)}, u32[]{:S(2)}, u32[]{:S(2)}) %all-to-all-start.8) | async-done | bytes 1179680 | tf_op jit(solution)/shard_map/all_to_all | solution.py:270
  679.8 32.5 %all_to_all.58 = bf16[8,2,36864]{2,1,0:T(2,128)(2,1)S(1)} all-to-all(bf16[8,2,36864]{2,1,0:T(2,128)(2,1)S(1)} %reshape.918), channel_id=1, replica_groups=mesh['expert'=8,'hidden'=4] {'expert'}, dimensions={0} | all-to-all | bytes 2359296 | tf_op jit(solution)/shard_map/all_to_all | solution.py:277
  712.3 208.9 %all-reduce.26.cloned.1.call-done = (bf16[8,384,768]{2,1,0:T(8,128)(2,1)}, bf16[8,384,768]{2,1,0:T(8,128)(2,1)}, bf16[8,384,768]{2,1,0:T(8,128)(2,1)}, bf16[8,384,768]{2,1,0:T(8,128)(2,1)}) async-done(((bf16[8,384,768]{2,1,0:T(8,128)(2,1)}, bf16[8,384,768]{2,1,0:T(8,128)(2,1)}, bf16[8,384,768]{2,1,0:T(8,128)(2,1)}, bf16[8,384,768]{2,1,0:T(8,128)(2,1)}), (bf16[8,384,768]{2,1,0:T(8,128)(2,1)}, ...) | async-done | bytes 18874384 | tf_op jit(solution)/shard_map/psum | solution.py:165
  921.3 110.1 %all_to_all.59 = bf16[8,384,768]{2,1,0:T(8,128)(2,1)} all-to-all(bf16[8,384,768]{2,1,0:T(8,128)(2,1)} %get-tuple-element.99), channel_id=1, replica_groups=mesh['expert'=8,'hidden'=4] {'expert'}, dimensions={0} | all-to-all | bytes 9437184 | tf_op jit(solution)/shard_map/all_to_all | solution.py:166
  1031.4 107.6 %all_to_all.60 = bf16[8,384,768]{2,1,0:T(8,128)(2,1)} all-to-all(bf16[8,384,768]{2,1,0:T(8,128)(2,1)S(1)} %copy-done.38), channel_id=1, replica_groups=mesh['expert'=8,'hidden'=4] {'expert'}, dimensions={0} | all-to-all | bytes 9437184 | tf_op jit(solution)/shard_map/all_to_all | solution.py:193
  1139.0 107.5 %all_to_all.61 = bf16[8,384,768]{2,1,0:T(8,128)(2,1)} all-to-all(bf16[8,384,768]{2,1,0:T(8,128)(2,1)S(1)} %bitcast.379), channel_id=1, replica_groups=mesh['expert'=8,'hidden'=4] {'expert'}, dimensions={0} | all-to-all | bytes 9437184 | tf_op jit(solution)/shard_map/all_to_all | solution.py:193
  1277.0 9.6 gather_fusion.5
  1286.6 9.6 gather_fusion.1
  1296.2 58.5 %all-to-all-done.3 = bf16[8,384,768]{2,1,0:T(8,128)(2,1)} async-done(((bf16[8,384,768]{2,1,0:T(8,128)(2,1)}), bf16[8,384,768]{2,1,0:T(8,128)(2,1)}, u32[]{:S(2)}, u32[]{:S(2)}) %all-to-all-start.3) | async-done | bytes 4718624 | tf_op jit(solution)/shard_map/all_to_all | solution.py:166
  1359.7 9.6 gather_fusion.7
  1369.3 9.6 gather_fusion.3
  1379.0 6.7 reshape.803
  1385.8 13.4 multiply_reduce_fusion.2
  1400.0 6.3 reshape.802
  1406.4 13.7 multiply_reduce_fusion.3
  1423.9 6.3 reshape.807
  1434.1 9.5 reduce_sum.493
  1443.6 9.3 reduce_sum.484
  1456.4 5.9 multiply_reduce_fusion.7
  1515.0 47.2 %all-reduce.24.cloned.1.call-done = (bf16[768,768]{1,0:T(8,128)(2,1)}, bf16[768,768]{1,0:T(8,128)(2,1)}) async-done(((bf16[768,768]{1,0:T(8,128)(2,1)}, bf16[768,768]{1,0:T(8,128)(2,1)}), (bf16[768,768]{1,0:T(8,128)(2,1)}, bf16[768,768]{1,0:T(8,128)(2,1)})) %all-reduce.24.cloned.1.call-update) | async-done | bytes 2359312 | tf_op jit(solution)/shard_map/psum | solution.py:255
  1570.1 38.8 %all-reduce.8 = (bf16[768]{0:T(1024)(128)(2,1)}, bf16[768]{0:T(1024)(128)(2,1)}, bf16[768]{0:T(1024)(128)(2,1)}, bf16[768]{0:T(1024)(128)(2,1)}, bf16[768,8]{0,1:T(8,128)(2,1)}) all-reduce(bf16[768]{0:T(1024)(128)(2,1)} %add_convert_fusion.6, ...), channel_id=1, replica_groups=mesh['expert'=8,'hidden'=4] {'expert'}, use_global_device_ids=true, to_apply=%region_56.57 | all-reduce | flops 9216 | bytes 36864 | tf_op jit(solution)/shard_map/psum | solution.py:261
  1617.8 29.0 %all-reduce.22.cloned.1.call-done = (bf16[3,768,192]{1,2,0:T(8,128)(2,1)}, bf16[192,768]{1,0:T(8,128)(2,1)}) async-done(((bf16[3,768,192]{1,2,0:T(8,128)(2,1)}, bf16[192,768]{1,0:T(8,128)(2,1)}), (bf16[3,768,192]{1,2,0:T(8,128)(2,1)}, bf16[192,768]{1,0:T(8,128)(2,1)})) %all-reduce.22.cloned.1.call-update) | async-done | bytes 1179664 | tf_op jit(solution)/shard_map/psum | solution.py:263
  (508 shorter events, 248.0 us)
Async XLA Ops:
  7.2 467.2 %copy-start = (bf16[1,768,768]{2,1,0:T(8,128)(2,1)S(1)}, bf16[1,768,768]{2,1,0:T(8,128)(2,1)}, u32[]{:S(2)}) copy-start(bf16[1,768,768]{2,1,0:T(8,128)(2,1)} %param.29) | copy-start | bytes 3538948
  7.2 57.4 %all-reduce.18.cloned.1.call-start = ((), (), s32[]{:S(2)}) async-start(), calls=%async_computation.10 | async-start | bytes 2359296 | tf_op jit(solution)/shard_map/psum | solution.py:143
  24.2 91.2 %all-reduce.20.cloned.1.call-start = ((), (), s32[]{:S(2)}) async-start(), calls=%async_computation.11 | async-start | bytes 2359296 | tf_op jit(solution)/shard_map/psum | solution.py:143
  26.0 97.0 %copy-start.102 = (s32[768,2]{0,1:T(2,128)}, s32[768,2]{0,1:T(2,128)S(1)}, u32[]{:S(2)}) copy-start(s32[768,2]{0,1:T(2,128)S(1)} %get-tuple-element.125) | copy-start | bytes 18436
  42.6 24.8 %copy-start.89 = (f32[768]{0:T(1024)}, f32[768]{0:T(1024)S(1)}, u32[]{:S(2)}) copy-start(f32[768]{0:T(1024)S(1)} %broadcast_multiply_fusion.3) | copy-start | bytes 9220
  88.1 17.2 %copy-start.138 = (f32[768]{0:T(1024)S(1)}, f32[768]{0:T(1024)}, u32[]{:S(2)}) copy-start(f32[768]{0:T(1024)} %get-tuple-element.75) | copy-start | bytes 9220
  105.3 14.0 copy-start.100
  142.7 9.1 copy-start.134
  142.7 110.0 %all-to-all-start.4 = ((bf16[8,384,768]{2,1,0:T(8,128)(2,1)}), bf16[8,384,768]{2,1,0:T(8,128)(2,1)}, u32[]{:S(2)}, u32[]{:S(2)}) async-start(bf16[8,384,768]{2,1,0:T(8,128)(2,1)} %bitcast.363), calls=%async_computation.4 | async-start | bytes 9437184 | tf_op jit(solution)/shard_map/all_to_all | solution.py:185
  148.4 11.4 copy-start.19
  252.7 108.5 %all-to-all-start.2 = ((bf16[8,384,768]{2,1,0:T(8,128)(2,1)}), bf16[8,384,768]{2,1,0:T(8,128)(2,1)}, u32[]{:S(2)}, u32[]{:S(2)}) async-start(bf16[8,384,768]{2,1,0:T(8,128)(2,1)} %bitcast.366), calls=%async_computation.2 | async-start | bytes 9437184 | tf_op jit(solution)/shard_map/all_to_all | solution.py:157
  361.2 108.5 %all-to-all-start = ((bf16[8,384,768]{2,1,0:T(8,128)(2,1)}), bf16[8,384,768]{2,1,0:T(8,128)(2,1)}, u32[]{:S(2)}, u32[]{:S(2)}) async-start(bf16[8,384,768]{2,1,0:T(8,128)(2,1)} %bitcast.364), calls=%async_computation | async-start | bytes 9437184 | tf_op jit(solution)/shard_map/all_to_all | solution.py:157
  369.7 7.0 copy-start.20
  369.7 7.0 copy-start.81
  369.7 7.4 copy-start.103
  469.6 108.3 %all-to-all-start.6 = ((bf16[8,384,768]{2,1,0:T(8,128)(2,1)}), bf16[8,384,768]{2,1,0:T(8,128)(2,1)}, u32[]{:S(2)}, u32[]{:S(2)}) async-start(bf16[8,384,768]{2,1,0:T(8,128)(2,1)} %bitcast.365), calls=%async_computation.6 | async-start | bytes 9437184 | tf_op jit(solution)/shard_map/all_to_all | solution.py:185
  474.3 447.0 %all-reduce.26.cloned.1.call-start = ((), (), s32[]{:S(2)}) async-start(), calls=%async_computation.14 | async-start | bytes 37748736 | tf_op jit(solution)/shard_map/psum | solution.py:165
  474.4 7.7 copy-start.142
  482.0 17.7 %copy-start.152 = (bf16[3072,768]{1,0:T(8,128)(2,1)}, bf16[3072,768]{1,0:T(8,128)(2,1)S(1)}, u32[]{:S(2)}) copy-start(bf16[3072,768]{1,0:T(8,128)(2,1)S(1)} %get-tuple-element.139) | copy-start | bytes 14155780
  617.1 33.9 %copy-start.34 = (f32[768,768]{1,0:T(8,128)S(1)}, f32[768,768]{1,0:T(8,128)}, u32[]{:S(2)}) copy-start(f32[768,768]{1,0:T(8,128)} %copy-done.33) | copy-start | bytes 7077892
  618.3 61.5 %all-to-all-start.8 = ((bf16[8,2,36864]{2,1,0:T(2,128)(2,1)}), bf16[8,2,36864]{2,1,0:T(2,128)(2,1)}, u32[]{:S(2)}, u32[]{:S(2)}) async-start(bf16[8,2,36864]{2,1,0:T(2,128)(2,1)} %reshape.916), calls=%async_computation.8 | async-start | bytes 2359296 | tf_op jit(solution)/shard_map/all_to_all | solution.py:270
  921.3 110.1 %copy-start.38 = (bf16[8,384,768]{2,1,0:T(8,128)(2,1)S(1)}, bf16[8,384,768]{2,1,0:T(8,128)(2,1)}, u32[]{:S(2)}) copy-start(bf16[8,384,768]{2,1,0:T(8,128)(2,1)} %get-tuple-element.100) | copy-start | bytes 14155780
  921.3 217.8 %slice-start.8 = ((s8[4718592]{0:T(1024)(128)(4,1)}), s8[4194304]{0:T(1024)(128)(4,1)S(1)}, s32[]{:S(2)}) async-start(s8[4718592]{0:T(1024)(128)(4,1)} %bitcast.378), calls=%async_computation.23 | async-start | bytes 8388608
  1031.4 107.6 %slice-start.9 = ((s8[4718592]{0:T(1024)(128)(4,1)}), s8[524288]{0:T(1024)(128)(4,1)S(1)}, s32[]{:S(2)}) async-start(s8[4718592]{0:T(1024)(128)(4,1)} %bitcast.378), calls=%async_computation.24 | async-start | bytes 1048576
  1246.5 108.2 %all-to-all-start.3 = ((bf16[8,384,768]{2,1,0:T(8,128)(2,1)}), bf16[8,384,768]{2,1,0:T(8,128)(2,1)}, u32[]{:S(2)}, u32[]{:S(2)}) async-start(bf16[8,384,768]{2,1,0:T(8,128)(2,1)} %get-tuple-element.98), calls=%async_computation.3 | async-start | bytes 9437184 | tf_op jit(solution)/shard_map/all_to_all | solution.py:166
  1251.3 310.9 %all-reduce.24.cloned.1.call-start = ((), (), s32[]{:S(2)}) async-start(), calls=%async_computation.13 | async-start | bytes 4718592 | tf_op jit(solution)/shard_map/psum | solution.py:255
  1258.4 13.6 slice-start.6
  1265.5 6.4 slice-start.7
  1266.6 7.8 slice-start.4
  1379.0 6.7 copy-start.14
  1379.0 6.7 copy-start.41
  1385.7 13.6 copy-start.73
  1385.7 13.6 copy-start.86
  1385.7 13.6 copy-start.99
  1385.8 13.7 copy-start.104
  1400.0 6.3 copy-start.12
  1406.4 14.9 copy-start.71
  1406.4 14.9 copy-start.84
  1406.4 14.9 copy-start.97
  1406.4 16.3 copy-start.24
  1423.8 6.3 copy-start.29
  1443.6 9.4 copy-start.82
  1443.6 12.7 copy-start.112
  1456.4 12.5 slice-start
  1462.4 6.5 slice-start.1
  1497.2 8.1 copy-start.67
  1498.6 6.7 copy-start.61
  1507.5 139.3 %all-reduce.22.cloned.1.call-start = ((), (), s32[]{:S(2)}) async-start(), calls=%async_computation.12 | async-start | bytes 2359296 | tf_op jit(solution)/shard_map/psum | solution.py:263
  (126 other events, 367.5 us)
Sparse Core Ops, SparseCore 0:
  24.3 40.3 all-reduce.17
  77.7 37.7 all-reduce.19
  601.2 320.0 all-reduce.25
  1507.6 54.4 all-reduce.23
  1566.1 80.6 all-reduce.21
where the time goes:
time: 1680 us; the launch traced here: 1670 us
  waiting for transfers between devices  693 us (41%)
  blocking collectives  397 us (24%)
  local copies, waits for them, and re-layouts  221 us (13%)
  other arithmetic  160 us (10%)
  matrix products  120 us (7%)
  starting transfers between devices  57.9 us (3%)
    all_to_all x2, blocking collectives, shards(): lax.all_to_all(in_summed.reshape(expert_count, capacity, feat_width), 'ex...  215 us
    psum x1, waiting for transfers between devices, shards(): summed = lax.psum(slice_out.astype(jnp.bfloat16), 'hidden')  209 us
    all_to_all x2, waiting for transfers between devices, shards(): lax.all_to_all(send_rows, 'expert', split_axis=0, concat_axis=0, tiled=True)  162 us
    all_to_all x2, waiting for transfers between devices, shards(): lax.all_to_all(send_grad, 'expert', split_axis=0, concat_axis=0, tiled=True)  141 us
    all_to_all x1, blocking collectives, shards(): lax.all_to_all(summed.reshape(expert_count, capacity, feat_width), 'exper...  110 us
    all_to_all x1, waiting for transfers between devices, shards(): lax.all_to_all(summed.reshape(expert_count, capacity, feat_width), 'exper...  58.5 us
    psum x1, waiting for transfers between devices, shards(): lax.psum(normed1_term.astype(jnp.bfloat16), 'hidden').astype(jnp.float32)  47.2 us
    psum x1, blocking collectives, shards(): lax.psum(gain1_total.astype(jnp.bfloat16), 'expert').astype(jnp.float32)  38.8 us
  transfers between devices with their start and end apart: 11, of which 11 were waited for; matrix products, arithmetic and copies ran while one was open for 15% of the time, Pallas kernels for 0%

commit v1 on v0

--- a/solution.py
+++ b/solution.py
@@ -267,12 +267,18 @@
         lax.psum(grad_router.astype(jnp.bfloat16), "expert").astype(jnp.float32),
     )
     expert_parts = (
-        lax.all_to_all(
-            expert_acc[0][None].astype(jnp.bfloat16),
-            "expert",
-            split_axis=1,
-            concat_axis=0,
-            tiled=True,
+        jnp.concatenate(
+            lax.all_to_all(
+                jnp.stack(
+                    jnp.split(
+                        expert_acc[0][None].astype(jnp.bfloat16), lax.axis_size("expert"), axis=1
+                    )
+                ),
+                "expert",
+                0,
+                0,
+            ),
+            axis=0,
         ).astype(jnp.float32),
         lax.all_to_all(
             expert_acc[1][None].astype(jnp.bfloat16),

time: 1680 us -> 1680 us (level)
    psum x2, waiting for transfers between devices: 28 us -> 5.17 us  [shards(): lax.psum(attn_term.astype(jnp.bfloat16), 'hidden').astype(jnp.float32)]
  transfers between devices with their start and end apart: 11 -> 11, of which waited for: 11 -> 10; matrix products, arithmetic and copies ran while one was open for 15% -> 15% of each run, Pallas kernels for 0% -> 0%
where the time goes in v1:
time: 1680 us; the launch traced here: 1670 us
  waiting for transfers between devices  699 us (42%)
  blocking collectives  397 us (24%)
  local copies, waits for them, and re-layouts  225 us (13%)
  other arithmetic  158 us (9%)
  matrix products  120 us (7%)
  starting transfers between devices  56.5 us (3%)
    all_to_all x2, blocking collectives, shards(): lax.all_to_all(in_summed.reshape(expert_count, capacity, feat_width), 'ex...  215 us
    psum x1, waiting for transfers between devices, shards(): summed = lax.psum(slice_out.astype(jnp.bfloat16), 'hidden')  214 us
    all_to_all x2, waiting for transfers between devices, shards(): lax.all_to_all(send_rows, 'expert', split_axis=0, concat_axis=0, tiled=True)  162 us
    all_to_all x2, waiting for transfers between devices, shards(): lax.all_to_all(send_grad, 'expert', split_axis=0, concat_axis=0, tiled=True)  153 us
    all_to_all x1, blocking collectives, shards(): lax.all_to_all(summed.reshape(expert_count, capacity, feat_width), 'exper...  110 us
    all_to_all x1, waiting for transfers between devices, shards(): lax.all_to_all(summed.reshape(expert_count, capacity, feat_width), 'exper...  65.8 us
    psum x1, waiting for transfers between devices, shards(): lax.psum(normed1_term.astype(jnp.bfloat16), 'hidden').astype(jnp.float32)  47.1 us
    psum x1, blocking collectives, shards(): lax.psum(gain1_total.astype(jnp.bfloat16), 'expert').astype(jnp.float32)  38.8 us
  transfers between devices with their start and end apart: 11, of which 10 were waited for; matrix products, arithmetic and copies ran while one was open for 15% of the time, Pallas kernels for 0%

profile of v1, /device:TPU:0, one launch (start us, length us, event | category | flops | bytes accessed | tf_op | source)
XLA Modules:
  0.0 1671.6 jit_solution(18171544478360142291)
XLA Ops:
  40.9 5.3 reduce-window.16
  85.6 5.5 mul.541
  91.1 6.9 mul.542
  98.6 6.9 scatter_custom_fusion
  107.5 7.3 scatter_custom_fusion.1
  116.1 5.2 all-reduce.20.cloned.1.call-done
  134.1 14.5 gather_fusion.4
  148.6 5.6 all-to-all-start.4
  154.4 14.5 gather_fusion.2
  168.9 89.7 %all-to-all-done.4 = bf16[8,384,768]{2,1,0:T(8,128)(2,1)} async-done(((bf16[8,384,768]{2,1,0:T(8,128)(2,1)}), bf16[8,384,768]{2,1,0:T(8,128)(2,1)}, u32[]{:S(2)}, u32[]{:S(2)}) %all-to-all-start.4) | async-done | bytes 4718624 | tf_op jit(solution)/shard_map/all_to_all | solution.py:185
  263.5 14.5 gather_fusion
  278.0 89.1 %all-to-all-done.2 = bf16[8,384,768]{2,1,0:T(8,128)(2,1)} async-done(((bf16[8,384,768]{2,1,0:T(8,128)(2,1)}), bf16[8,384,768]{2,1,0:T(8,128)(2,1)}, u32[]{:S(2)}, u32[]{:S(2)}) %all-to-all-start.2) | async-done | bytes 4718624 | tf_op jit(solution)/shard_map/all_to_all | solution.py:157
  375.7 7.0 mul.579
  388.1 14.6 gather_fusion.6
  402.7 72.9 %all-to-all-done = bf16[8,384,768]{2,1,0:T(8,128)(2,1)} async-done(((bf16[8,384,768]{2,1,0:T(8,128)(2,1)}), bf16[8,384,768]{2,1,0:T(8,128)(2,1)}, u32[]{:S(2)}, u32[]{:S(2)}) %all-to-all-start) | async-done | bytes 4718624 | tf_op jit(solution)/shard_map/all_to_all | solution.py:157
  480.2 7.5 multiply_convert_fusion.1
  487.8 12.1 fusion.7
  499.9 5.5 convolution_convert_fusion.1
  505.4 5.5 convolution_convert_fusion.3
  511.0 10.1 multiply_convert_fusion
  521.1 62.8 %all-to-all-done.6 = bf16[8,384,768]{2,1,0:T(8,128)(2,1)} async-done(((bf16[8,384,768]{2,1,0:T(8,128)(2,1)}), bf16[8,384,768]{2,1,0:T(8,128)(2,1)}, u32[]{:S(2)}, u32[]{:S(2)}) %all-to-all-start.6) | async-done | bytes 4718624 | tf_op jit(solution)/shard_map/all_to_all | solution.py:185
  583.9 12.1 fusion.14
  596.1 5.6 convolution_convert_fusion
  601.7 5.6 convolution_convert_fusion.2
  611.5 7.8 reduce.30
  620.5 31.6 %all-to-all-start.9 = ((bf16[8,2,36864]{2,1,0:T(2,128)(2,1)}), bf16[8,2,36864]{2,1,0:T(2,128)(2,1)S(1)}, u32[]{:S(2)}, u32[]{:S(2)}) async-start(bf16[8,2,36864]{2,1,0:T(2,128)(2,1)} %reshape.921), calls=%async_computation.9 | async-start | bytes 2359296 | tf_op jit(solution)/shard_map/all_to_all | solution.py:283
  657.5 23.4 %all-to-all-done.9 = bf16[8,2,36864]{2,1,0:T(2,128)(2,1)S(1)} async-done(((bf16[8,2,36864]{2,1,0:T(2,128)(2,1)}), bf16[8,2,36864]{2,1,0:T(2,128)(2,1)S(1)}, u32[]{:S(2)}, u32[]{:S(2)}) %all-to-all-start.9) | async-done | bytes 1179680 | tf_op jit(solution)/shard_map/all_to_all | solution.py:283
  680.9 32.7 %all_to_all.54 = bf16[8,1,96,768]{3,2,1,0:T(8,128)(2,1)S(1)} all-to-all(bf16[8,1,96,768]{3,2,1,0:T(8,128)(2,1)} %constant_dynamic-update-slice_fusion), channel_id=1, replica_groups=mesh['expert'=8,'hidden'=4] {'expert'}, dimensions={0} | all-to-all | bytes 2359296 | tf_op jit(solution)/shard_map/all_to_all | solution.py:271
  713.6 213.8 %all-reduce.26.cloned.1.call-done = (bf16[8,384,768]{2,1,0:T(8,128)(2,1)}, bf16[8,384,768]{2,1,0:T(8,128)(2,1)}, bf16[8,384,768]{2,1,0:T(8,128)(2,1)}, bf16[8,384,768]{2,1,0:T(8,128)(2,1)}) async-done(((bf16[8,384,768]{2,1,0:T(8,128)(2,1)}, bf16[8,384,768]{2,1,0:T(8,128)(2,1)}, bf16[8,384,768]{2,1,0:T(8,128)(2,1)}, bf16[8,384,768]{2,1,0:T(8,128)(2,1)}), (bf16[8,384,768]{2,1,0:T(8,128)(2,1)}, ...) | async-done | bytes 18874384 | tf_op jit(solution)/shard_map/psum | solution.py:165
  927.4 110.1 %all_to_all.55 = bf16[8,384,768]{2,1,0:T(8,128)(2,1)} all-to-all(bf16[8,384,768]{2,1,0:T(8,128)(2,1)} %get-tuple-element.206), channel_id=1, replica_groups=mesh['expert'=8,'hidden'=4] {'expert'}, dimensions={0} | all-to-all | bytes 9437184 | tf_op jit(solution)/shard_map/all_to_all | solution.py:166
  1037.6 107.6 %all_to_all.56 = bf16[8,384,768]{2,1,0:T(8,128)(2,1)} all-to-all(bf16[8,384,768]{2,1,0:T(8,128)(2,1)S(1)} %copy-done.39), channel_id=1, replica_groups=mesh['expert'=8,'hidden'=4] {'expert'}, dimensions={0} | all-to-all | bytes 9437184 | tf_op jit(solution)/shard_map/all_to_all | solution.py:193
  1145.2 107.5 %all_to_all.57 = bf16[8,384,768]{2,1,0:T(8,128)(2,1)} all-to-all(bf16[8,384,768]{2,1,0:T(8,128)(2,1)S(1)} %bitcast.411), channel_id=1, replica_groups=mesh['expert'=8,'hidden'=4] {'expert'}, dimensions={0} | all-to-all | bytes 9437184 | tf_op jit(solution)/shard_map/all_to_all | solution.py:193
  1275.8 9.6 gather_fusion.5
  1285.5 9.7 gather_fusion.1
  1295.2 65.8 %all-to-all-done.3 = bf16[8,384,768]{2,1,0:T(8,128)(2,1)} async-done(((bf16[8,384,768]{2,1,0:T(8,128)(2,1)}), bf16[8,384,768]{2,1,0:T(8,128)(2,1)}, u32[]{:S(2)}, u32[]{:S(2)}) %all-to-all-start.3) | async-done | bytes 4718624 | tf_op jit(solution)/shard_map/all_to_all | solution.py:166
  1365.9 9.6 gather_fusion.7
  1375.5 9.6 gather_fusion.3
  1385.2 6.3 reshape.808
  1391.6 13.8 multiply_reduce_fusion.2
  1406.2 6.3 reshape.807
  1412.6 13.7 multiply_reduce_fusion.3
  1430.0 6.3 reshape.812
  1440.2 9.5 reduce_sum.493
  1449.7 9.3 reduce_sum.484
  1462.6 5.9 multiply_reduce_fusion.7
  1521.2 47.1 %all-reduce.24.cloned.1.call-done = (bf16[768,768]{1,0:T(8,128)(2,1)}, bf16[768,768]{1,0:T(8,128)(2,1)}) async-done(((bf16[768,768]{1,0:T(8,128)(2,1)}, bf16[768,768]{1,0:T(8,128)(2,1)}), (bf16[768,768]{1,0:T(8,128)(2,1)}, bf16[768,768]{1,0:T(8,128)(2,1)})) %all-reduce.24.cloned.1.call-update) | async-done | bytes 2359312 | tf_op jit(solution)/shard_map/psum | solution.py:255
  1576.2 38.8 %all-reduce.8 = (bf16[768]{0:T(1024)(128)(2,1)}, bf16[768]{0:T(1024)(128)(2,1)}, bf16[768]{0:T(1024)(128)(2,1)}, bf16[768]{0:T(1024)(128)(2,1)}, bf16[768,8]{0,1:T(8,128)(2,1)}) all-reduce(bf16[768]{0:T(1024)(128)(2,1)} %add_convert_fusion.7, ...), channel_id=1, replica_groups=mesh['expert'=8,'hidden'=4] {'expert'}, use_global_device_ids=true, to_apply=%region_56.57 | all-reduce | flops 9216 | bytes 36864 | tf_op jit(solution)/shard_map/psum | solution.py:261
  1623.9 29.2 %all-reduce.22.cloned.1.call-done = (bf16[3,768,192]{1,2,0:T(8,128)(2,1)}, bf16[192,768]{1,0:T(8,128)(2,1)}) async-done(((bf16[3,768,192]{1,2,0:T(8,128)(2,1)}, bf16[192,768]{1,0:T(8,128)(2,1)}), (bf16[3,768,192]{1,2,0:T(8,128)(2,1)}, bf16[192,768]{1,0:T(8,128)(2,1)})) %all-reduce.22.cloned.1.call-update) | async-done | bytes 1179664 | tf_op jit(solution)/shard_map/psum | solution.py:263
  (537 shorter events, 244.2 us)
Async XLA Ops:
  7.2 473.0 %copy-start = (bf16[1,768,768]{2,1,0:T(8,128)(2,1)S(1)}, bf16[1,768,768]{2,1,0:T(8,128)(2,1)}, u32[]{:S(2)}) copy-start(bf16[1,768,768]{2,1,0:T(8,128)(2,1)} %param.29) | copy-start | bytes 3538948
  7.2 60.7 %all-reduce.18.cloned.1.call-start = ((), (), s32[]{:S(2)}) async-start(), calls=%async_computation.10 | async-start | bytes 2359296 | tf_op jit(solution)/shard_map/psum | solution.py:143
  24.2 97.1 %all-reduce.20.cloned.1.call-start = ((), (), s32[]{:S(2)}) async-start(), calls=%async_computation.11 | async-start | bytes 2359296 | tf_op jit(solution)/shard_map/psum | solution.py:143
  25.6 103.4 %copy-start.119 = (s32[768,2]{0,1:T(2,128)}, s32[768,2]{0,1:T(2,128)S(1)}, u32[]{:S(2)}) copy-start(s32[768,2]{0,1:T(2,128)S(1)} %get-tuple-element.248) | copy-start | bytes 18436
  63.8 6.9 copy-start.106
  91.1 25.0 %copy-start.153 = (f32[768]{0:T(1024)S(1)}, f32[768]{0:T(1024)}, u32[]{:S(2)}) copy-start(f32[768]{0:T(1024)} %get-tuple-element.182) | copy-start | bytes 9220
  116.1 9.1 copy-start.117
  148.6 110.0 %all-to-all-start.4 = ((bf16[8,384,768]{2,1,0:T(8,128)(2,1)}), bf16[8,384,768]{2,1,0:T(8,128)(2,1)}, u32[]{:S(2)}, u32[]{:S(2)}) async-start(bf16[8,384,768]{2,1,0:T(8,128)(2,1)} %bitcast.400), calls=%async_computation.4 | async-start | bytes 9437184 | tf_op jit(solution)/shard_map/all_to_all | solution.py:185
  258.6 108.5 %all-to-all-start.2 = ((bf16[8,384,768]{2,1,0:T(8,128)(2,1)}), bf16[8,384,768]{2,1,0:T(8,128)(2,1)}, u32[]{:S(2)}, u32[]{:S(2)}) async-start(bf16[8,384,768]{2,1,0:T(8,128)(2,1)} %bitcast.399), calls=%async_computation.2 | async-start | bytes 9437184 | tf_op jit(solution)/shard_map/all_to_all | solution.py:157
  367.1 108.5 %all-to-all-start = ((bf16[8,384,768]{2,1,0:T(8,128)(2,1)}), bf16[8,384,768]{2,1,0:T(8,128)(2,1)}, u32[]{:S(2)}, u32[]{:S(2)}) async-start(bf16[8,384,768]{2,1,0:T(8,128)(2,1)} %bitcast.397), calls=%async_computation | async-start | bytes 9437184 | tf_op jit(solution)/shard_map/all_to_all | solution.py:157
  375.7 7.0 copy-start.21
  375.7 7.0 copy-start.98
  375.7 7.4 copy-start.120
  475.6 108.3 %all-to-all-start.6 = ((bf16[8,384,768]{2,1,0:T(8,128)(2,1)}), bf16[8,384,768]{2,1,0:T(8,128)(2,1)}, u32[]{:S(2)}, u32[]{:S(2)}) async-start(bf16[8,384,768]{2,1,0:T(8,128)(2,1)} %bitcast.398), calls=%async_computation.6 | async-start | bytes 9437184 | tf_op jit(solution)/shard_map/all_to_all | solution.py:185
  480.2 447.3 %all-reduce.26.cloned.1.call-start = ((), (), s32[]{:S(2)}) async-start(), calls=%async_computation.14 | async-start | bytes 37748736 | tf_op jit(solution)/shard_map/psum | solution.py:165
  480.2 7.6 copy-start.157
  487.8 17.6 %copy-start.167 = (bf16[3072,768]{1,0:T(8,128)(2,1)}, bf16[3072,768]{1,0:T(8,128)(2,1)S(1)}, u32[]{:S(2)}) copy-start(bf16[3072,768]{1,0:T(8,128)(2,1)S(1)} %get-tuple-element.262) | copy-start | bytes 14155780
  619.3 32.8 %copy-start.76 = (bf16[1,1,96,768]{3,2,1,0:T(8,128)(2,1)S(1)}, bf16[1,1,96,768]{3,2,1,0:T(8,128)(2,1)}, u32[]{:S(2)}) copy-start(bf16[1,1,96,768]{3,2,1,0:T(8,128)(2,1)} %copy-done.75) | copy-start | bytes 442372
  619.3 33.5 %copy-start.74 = (bf16[1,1,96,768]{3,2,1,0:T(8,128)(2,1)S(1)}, bf16[1,1,96,768]{3,2,1,0:T(8,128)(2,1)}, u32[]{:S(2)}) copy-start(bf16[1,1,96,768]{3,2,1,0:T(8,128)(2,1)} %copy-done.73) | copy-start | bytes 442372
  619.3 34.1 %copy-start.72 = (bf16[1,1,96,768]{3,2,1,0:T(8,128)(2,1)S(1)}, bf16[1,1,96,768]{3,2,1,0:T(8,128)(2,1)}, u32[]{:S(2)}) copy-start(bf16[1,1,96,768]{3,2,1,0:T(8,128)(2,1)} %copy-done.71) | copy-start | bytes 442372
  619.4 34.8 %copy-start.70 = (bf16[1,1,96,768]{3,2,1,0:T(8,128)(2,1)S(1)}, bf16[1,1,96,768]{3,2,1,0:T(8,128)(2,1)}, u32[]{:S(2)}) copy-start(bf16[1,1,96,768]{3,2,1,0:T(8,128)(2,1)} %copy-done.69) | copy-start | bytes 442372
  620.5 34.3 %copy-start.68 = (bf16[1,1,96,768]{3,2,1,0:T(8,128)(2,1)S(1)}, bf16[1,1,96,768]{3,2,1,0:T(8,128)(2,1)}, u32[]{:S(2)}) copy-start(bf16[1,1,96,768]{3,2,1,0:T(8,128)(2,1)} %copy-done.67) | copy-start | bytes 442372
  620.5 35.0 %copy-start.66 = (bf16[1,1,96,768]{3,2,1,0:T(8,128)(2,1)S(1)}, bf16[1,1,96,768]{3,2,1,0:T(8,128)(2,1)}, u32[]{:S(2)}) copy-start(bf16[1,1,96,768]{3,2,1,0:T(8,128)(2,1)} %copy-done.65) | copy-start | bytes 442372
  620.5 35.6 %copy-start.64 = (bf16[1,1,96,768]{3,2,1,0:T(8,128)(2,1)S(1)}, bf16[1,1,96,768]{3,2,1,0:T(8,128)(2,1)}, u32[]{:S(2)}) copy-start(bf16[1,1,96,768]{3,2,1,0:T(8,128)(2,1)} %copy-done.63) | copy-start | bytes 442372
  620.5 36.3 %copy-start.62 = (bf16[1,1,96,768]{3,2,1,0:T(8,128)(2,1)S(1)}, bf16[1,1,96,768]{3,2,1,0:T(8,128)(2,1)}, u32[]{:S(2)}) copy-start(bf16[1,1,96,768]{3,2,1,0:T(8,128)(2,1)} %copy-done.61) | copy-start | bytes 442372
  620.5 60.4 %all-to-all-start.9 = ((bf16[8,2,36864]{2,1,0:T(2,128)(2,1)}), bf16[8,2,36864]{2,1,0:T(2,128)(2,1)S(1)}, u32[]{:S(2)}, u32[]{:S(2)}) async-start(bf16[8,2,36864]{2,1,0:T(2,128)(2,1)} %reshape.921), calls=%async_computation.9 | async-start | bytes 2359296 | tf_op jit(solution)/shard_map/all_to_all | solution.py:283
  927.4 110.1 %copy-start.39 = (bf16[8,384,768]{2,1,0:T(8,128)(2,1)S(1)}, bf16[8,384,768]{2,1,0:T(8,128)(2,1)}, u32[]{:S(2)}) copy-start(bf16[8,384,768]{2,1,0:T(8,128)(2,1)} %get-tuple-element.207) | copy-start | bytes 14155780
  927.4 217.8 %slice-start.8 = ((s8[4718592]{0:T(1024)(128)(4,1)}), s8[4194304]{0:T(1024)(128)(4,1)S(1)}, s32[]{:S(2)}) async-start(s8[4718592]{0:T(1024)(128)(4,1)} %bitcast.410), calls=%async_computation.23 | async-start | bytes 8388608
  1037.6 107.6 %slice-start.9 = ((s8[4718592]{0:T(1024)(128)(4,1)}), s8[524288]{0:T(1024)(128)(4,1)S(1)}, s32[]{:S(2)}) async-start(s8[4718592]{0:T(1024)(128)(4,1)} %bitcast.410), calls=%async_computation.24 | async-start | bytes 1048576
  1252.7 108.3 %all-to-all-start.3 = ((bf16[8,384,768]{2,1,0:T(8,128)(2,1)}), bf16[8,384,768]{2,1,0:T(8,128)(2,1)}, u32[]{:S(2)}, u32[]{:S(2)}) async-start(bf16[8,384,768]{2,1,0:T(8,128)(2,1)} %get-tuple-element.205), calls=%async_computation.3 | async-start | bytes 9437184 | tf_op jit(solution)/shard_map/all_to_all | solution.py:166
  1257.5 310.9 %all-reduce.24.cloned.1.call-start = ((), (), s32[]{:S(2)}) async-start(), calls=%async_computation.13 | async-start | bytes 4718592 | tf_op jit(solution)/shard_map/psum | solution.py:255
  1259.0 11.1 slice-start.6
  1385.2 6.4 copy-start.42
  1391.5 14.0 copy-start.90
  1391.5 14.0 copy-start.103
  1391.5 14.0 copy-start.116
  1391.5 14.1 copy-start.121
  1412.6 14.8 copy-start.88
  1412.6 14.8 copy-start.101
  1412.6 14.8 copy-start.114
  1412.6 16.2 copy-start.25
  1449.7 9.4 copy-start.99
  1449.7 12.7 copy-start.129
  1462.5 12.5 slice-start
  1468.6 6.5 slice-start.1
  1503.4 8.1 copy-start.84
  1504.8 6.7 copy-start.78
  1513.7 139.4 %all-reduce.22.cloned.1.call-start = ((), (), s32[]{:S(2)}) async-start(), calls=%async_computation.12 | async-start | bytes 2359296 | tf_op jit(solution)/shard_map/psum | solution.py:263
  (139 other events, 407.9 us)
Sparse Core Ops, SparseCore 0:
  24.3 40.3 all-reduce.17
  80.9 40.2 all-reduce.19
  607.4 320.0 all-reduce.25
  1513.8 54.4 all-reduce.23
  1572.3 80.7 all-reduce.21
